TPU v7x, 256 devices: a whole 4x4x8 slice. The times are simulated.
256 devices in a mesh: dp: 32 (over y, x, core), expert: 8 (over z).
Axes of the slice: x: 4, y: 4, z: 8, core: 2. Of those that a mesh axis runs over, the one named last changes fastest.
Arguments:
- tokens: bfloat16 [4096, 2048], P('dp'), may hold values from -6 to 6
- route_expert: int32 [4096, 4], P('dp'), may hold values from 0 to 31, all different within a row; in each aligned block of 128 rows (0 to 127, 128 to 255, ...) at most 32 rows name the same one
- route_weight: float32 [4096, 4], P('dp'), may hold values from 0.1 to 1
- gate_weight: bfloat16 [32, 1408, 2048], P('dp', 'expert'), may hold values from -0.125 to 0.125
- up_weight: bfloat16 [32, 1408, 2048], P('dp', 'expert'), may hold values from -0.125 to 0.125
- down_weight: bfloat16 [32, 1408, 2048], P('dp', 'expert'), may hold values from -0.15625 to 0.15625
- gate_scale: float32 [32, 1408], P('dp', 'expert'), may hold values from 0.5 to 2
- up_scale: float32 [32, 1408], P('dp', 'expert'), may hold values from 0.5 to 2
- down_scale: float32 [32, 2048], replicated, may hold values from 0.5 to 2
- cotangent: bfloat16 [4096, 2048], P('dp', 'expert'), may hold values from -6 to 6
Outputs:
- mixed: bfloat16 [4096, 2048], P('dp', 'expert')
- token_grad: bfloat16 [4096, 2048], P('dp', 'expert')
- route_grad: float32 [4096, 4], P('dp')
- gate_grad: float32 [32, 1408, 2048], P('dp', 'expert')
- up_grad: float32 [32, 1408, 2048], P('dp', 'expert')
- down_grad: float32 [32, 1408, 2048], P('dp', 'expert')
Inputs may be any that keep to these rules, and one draw needn't show every extreme that they name: `route_expert`: each row names 4 different experts. Among the 128 rows of one aligned block (the tokens of one index of dp) no expert is named by more than 32 rows, and in some block one expert is named by exactly 32 rows.
All inputs are finite; a program needn't handle non-finite values.
Results may differ from a plain program's by a relative error of at most 0.0058.
Values may be sent and summed in bfloat16 or wider, within the bound.
No kernel may reach another device: no remote copies, remote signals or barrier semaphores. Data moves between devices by JAX's collectives and lax.ppermute only.
A program may use at most 128 MiB of HBM per device.

v0:
```python
import jax
import jax.numpy as jnp
from jax import lax
from jax.sharding import PartitionSpec as P


def local(
    tokens,
    route_expert,
    route_weight,
    gate_weight,
    up_weight,
    down_weight,
    gate_scale,
    up_scale,
    down_scale,
    cotangent,
):
    owners = lax.axis_size("dp")
    tok_rows, width = tokens.shape
    choose = route_expert.shape[1]
    capacity = 2 * tok_rows * choose // owners
    slots = owners * capacity
    assigned = tok_rows * choose
    col_share = width // lax.axis_size("expert")
    col_start = lax.axis_index("expert") * col_share
    flat_expert = route_expert.reshape(-1)
    one_hot = (flat_expert[:, None] == jnp.arange(owners, dtype=jnp.int32)[None, :]).astype(
        jnp.int32
    )
    ranks = jnp.sum((jnp.cumsum(one_hot, axis=0) - 1) * one_hot, axis=1)
    slot_index = flat_expert * capacity + ranks
    slot_token = (
        jnp.zeros((slots,), jnp.int32)
        .at[slot_index]
        .set(jnp.arange(assigned, dtype=jnp.int32) // choose)
    )
    filled = jnp.zeros((slots,), jnp.bool_).at[slot_index].set(True)
    slot_weight = jnp.zeros((slots,), jnp.float32).at[slot_index].set(route_weight.reshape(-1))
    outgoing = jnp.where(
        filled[:, None], jnp.take(tokens, slot_token, axis=0), jnp.zeros((), tokens.dtype)
    )
    arrived = lax.all_to_all(
        outgoing.reshape(owners, capacity, width), "dp", split_axis=0, concat_axis=0, tiled=True
    ).reshape(slots, width)
    gate_local = gate_weight[0]
    up_local = up_weight[0]
    down_local = down_weight[0]
    gate_pre = (
        lax.dot_general(
            arrived, gate_local, (((1,), (1,)), ((), ())), preferred_element_type=jnp.float32
        )
        * gate_scale[0][None, :]
    )
    up_pre = (
        lax.dot_general(
            arrived, up_local, (((1,), (1,)), ((), ())), preferred_element_type=jnp.float32
        )
        * up_scale[0][None, :]
    )
    sigmoid_gate = jax.nn.sigmoid(gate_pre)
    silu_gate = gate_pre * sigmoid_gate
    hidden = (silu_gate * up_pre).astype(jnp.bfloat16)
    summed = lax.psum_scatter(
        lax.dot_general(
            down_local, hidden, (((0,), (1,)), ((), ())), preferred_element_type=jnp.float32
        ),
        "expert",
        scatter_dimension=0,
        tiled=True,
    )
    owner_scale = lax.dynamic_slice(down_scale, (lax.axis_index("dp"), col_start), (1, col_share))[
        0
    ]
    out_cols = (summed * owner_scale[:, None]).astype(jnp.bfloat16)
    returned = lax.all_to_all(
        out_cols.reshape(col_share, owners, capacity), "dp", split_axis=1, concat_axis=1, tiled=True
    ).reshape(col_share, slots)
    picked = (
        jnp.take(returned, slot_index, axis=1)
        .reshape(col_share, tok_rows, choose)
        .astype(jnp.float32)
    )
    mixed = jnp.sum(picked * route_weight[None, :, :], axis=2).T.astype(jnp.bfloat16)
    cot_cols = cotangent.T.astype(jnp.float32)
    route_part = jnp.sum(picked * cot_cols[:, :, None], axis=0)
    route_grad = lax.psum(route_part, "expert")
    slot_scale = jnp.repeat(down_scale, capacity, axis=0)
    full_cot = lax.all_gather(cotangent, "expert", axis=1, tiled=True)
    cot_slots = jnp.take(full_cot, slot_token, axis=0).astype(jnp.float32)
    weighted = (cot_slots * slot_weight[:, None] * slot_scale).astype(jnp.bfloat16)
    out_grad = lax.all_to_all(
        weighted.reshape(owners, capacity, width), "dp", split_axis=0, concat_axis=0, tiled=True
    ).reshape(slots, width)
    hidden_grad = lax.dot_general(
        out_grad, down_local, (((1,), (1,)), ((), ())), preferred_element_type=jnp.float32
    )
    gate_in = (
        hidden_grad
        * up_pre
        * sigmoid_gate
        * (1.0 + gate_pre * (1.0 - sigmoid_gate))
        * gate_scale[0][None, :]
    ).astype(jnp.bfloat16)
    up_in = (hidden_grad * silu_gate * up_scale[0][None, :]).astype(jnp.bfloat16)
    down_grad = lax.dot_general(
        hidden, out_grad, (((0,), (0,)), ((), ())), preferred_element_type=jnp.float32
    )
    gate_grad = lax.dot_general(
        gate_in, arrived, (((0,), (0,)), ((), ())), preferred_element_type=jnp.float32
    )
    up_grad = lax.dot_general(
        up_in, arrived, (((0,), (0,)), ((), ())), preferred_element_type=jnp.float32
    )
    first = lax.dot_general(
        gate_local, gate_in, (((0,), (1,)), ((), ())), preferred_element_type=jnp.float32
    )
    second = lax.dot_general(
        up_local, up_in, (((0,), (1,)), ((), ())), preferred_element_type=jnp.float32
    )
    input_cols = lax.psum_scatter(first + second, "expert", scatter_dimension=0, tiled=True)
    input_home = lax.all_to_all(
        input_cols.reshape(col_share, owners, capacity),
        "dp",
        split_axis=1,
        concat_axis=1,
        tiled=True,
    ).reshape(col_share, slots)
    token_grad = jnp.sum(
        jnp.take(input_home, slot_index, axis=1).reshape(col_share, tok_rows, choose), axis=2
    ).T.astype(jnp.bfloat16)
    return (mixed, token_grad, route_grad, gate_grad[None], up_grad[None], down_grad[None])


def solution(mesh):
    return jax.shard_map(
        local,
        mesh=mesh,
        in_specs=(
            P("dp", None),
            P("dp", None),
            P("dp", None),
            P("dp", "expert", None),
            P("dp", "expert", None),
            P("dp", "expert", None),
            P("dp", "expert"),
            P("dp", "expert"),
            P(),
            P("dp", "expert"),
        ),
        out_specs=(
            P("dp", "expert"),
            P("dp", "expert"),
            P("dp", None),
            P("dp", "expert", None),
            P("dp", "expert", None),
            P("dp", "expert", None),
        ),
        check_vma=False,
    )
```

profile of v0, /device:TPU:2, one launch (start us, length us, event | category | flops | bytes accessed | tf_op | source)
XLA Modules:
  0.0 436.8 jit_solution(8157642740581195982)
XLA Ops:
  7.2 0.0 copy-start
  7.2 0.9 copy.18
  8.0 0.1 eq.26
  8.2 0.1 reshape.136
  8.3 1.2 reduce-window.6
  9.5 0.2 slice_reduce_fusion
  9.7 0.1 mul.123
  9.8 0.1 fusion.11
  10.0 2.4 scatter_custom_fusion.1
  12.4 0.8 copy.22
  13.2 0.1 reshape.200
  13.3 29.3 %all_gather.3 = bf16[128,2048]{1,0:T(8,128)(2,1)S(1)} all-gather(bf16[128,256]{1,0:T(8,128)(2,1)} %param.21), channel_id=1, replica_groups=mesh['dp'=32,'expert'=8] {'expert'}, dimensions={1}, use_global_device_ids=true | all-gather | bytes 589824 | tf_op jit(solution)/shard_map/all_gather | solution.py:89
  42.7 2.4 scatter_custom_fusion.2
  45.1 0.0 copy-start.7
  45.1 6.0 %gather_fusion.3 = bf16[1024,2048]{1,0:T(8,128)(2,1)} fusion(bf16[128,2048]{1,0:T(8,128)(2,1)S(1)} %all_gather.3, s32[1024]{0:T(1024)S(1)} %fusion.13), kind=kCustom, calls=%fused_computation.1.clone | custom fusion | bytes 8392704 | tf_op jit(solution)/shard_map/jit(_take)/gather | solution.py:90
  51.2 0.0 copy-done.7
  51.2 4.5 %fusion = bf16[1024,2048]{1,0:T(8,128)(2,1)} fusion(bf16[1024,2048]{1,0:T(8,128)(2,1)} %gather_fusion.3, f32[32,2048]{1,0:T(8,128)S(1)} %copy-done.7, f32[1024]{0:T(1024)S(1)} %scatter_custom_fusion.2, pred[1024]{0:T(1024)(128)(4,1)S(1)} %compare_and_fusion.1), kind=kLoop, calls=%fused_computation.8 | loop fusion | flops 10485760 | bytes 8655872 | tf_op jit(solution)/shard_map/convert_element_type | solution.py:91
  55.6 7.8 %all-to-all-start.2 = ((bf16[32,32,2048]{2,1,0:T(8,128)(2,1)}), bf16[32,32,2048]{2,1,0:T(8,128)(2,1)}, u32[]{:S(2)}, u32[]{:S(2)}) async-start(bf16[32,32,2048]{2,1,0:T(8,128)(2,1)} %bitcast.93), calls=%async_computation.3 | async-start | bytes 8388608 | tf_op jit(solution)/shard_map/all_to_all | solution.py:92
  63.4 0.0 copy-done.1
  63.4 6.0 %gather_fusion.2 = bf16[1024,2048]{1,0:T(8,128)(2,1)} fusion(bf16[128,2048]{1,0:T(8,128)(2,1)S(1)} %copy-done.1, s32[1024]{0:T(1024)S(1)} %fusion.13), kind=kCustom, calls=%fused_computation.clone | custom fusion | bytes 8392704 | tf_op jit(solution)/shard_map/jit(_take)/gather | solution.py:41
  69.5 2.4 scatter_custom_fusion
  71.9 4.0 select_select_fusion
  75.9 38.9 %all-to-all-done.2 = bf16[32,32,2048]{2,1,0:T(8,128)(2,1)} async-done(((bf16[32,32,2048]{2,1,0:T(8,128)(2,1)}), bf16[32,32,2048]{2,1,0:T(8,128)(2,1)}, u32[]{:S(2)}, u32[]{:S(2)}) %all-to-all-start.2) | async-done | bytes 4194336 | tf_op jit(solution)/shard_map/all_to_all | solution.py:92
  114.9 7.4 %all-to-all-start = ((bf16[32,32,2048]{2,1,0:T(8,128)(2,1)}), bf16[32,32,2048]{2,1,0:T(8,128)(2,1)}, u32[]{:S(2)}, u32[]{:S(2)}) async-start(bf16[32,32,2048]{2,1,0:T(8,128)(2,1)} %bitcast.92), calls=%async_computation | async-start | bytes 8388608 | tf_op jit(solution)/shard_map/all_to_all | solution.py:43
  122.3 0.0 copy-start.6
  122.3 0.0 copy-start.9
  122.3 0.2 reduce-scatter.3.cloned.1.call-start
  122.5 4.6 %fusion.1 = f32[1024,176]{0,1:T(8,128)} fusion(bf16[1024,2048]{1,0:T(8,128)(2,1)} %bitcast.18, bf16[1,176,2048]{2,1,0:T(8,128)(2,1)S(1)} %copy-done.5), kind=kOutput, calls=%fused_computation.18 | convolution fusion | flops 738197504 | bytes 5636096 | tf_op jit(solution)/shard_map/dot_general | solution.py:95
  127.1 46.7 %all-to-all-done = bf16[32,32,2048]{2,1,0:T(8,128)(2,1)} async-done(((bf16[32,32,2048]{2,1,0:T(8,128)(2,1)}), bf16[32,32,2048]{2,1,0:T(8,128)(2,1)}, u32[]{:S(2)}, u32[]{:S(2)}) %all-to-all-start) | async-done | bytes 4194336 | tf_op jit(solution)/shard_map/all_to_all | solution.py:43
  173.8 3.8 convolution_multiply_fusion.1
  177.6 4.0 multiply_convert_fusion.3
  181.7 0.0 copy-start.2
  181.7 0.0 copy-start.3
  181.7 0.7 copy-done.2
  182.4 4.5 %convolution_bitcast_fusion = f32[2048,1024]{0,1:T(8,128)} fusion(bf16[1024,176]{0,1:T(8,128)(2,1)S(1)} %get-tuple-element.15, bf16[1,176,2048]{2,1,0:T(8,128)(2,1)S(1)} %copy-done.5), kind=kOutput, calls=%fused_computation.10 | convolution fusion | flops 738197504 | bytes 9469952 | tf_op jit(solution)/shard_map/dot_general | solution.py:65
  186.9 0.0 reduce-scatter.3.cloned.1.call-update
  186.9 0.0 reduce-scatter.5.cloned.1.call-start
  187.0 1.3 fusion.6
  188.3 4.5 %add_bitcast_fusion = f32[2048,1024]{0,1:T(8,128)} fusion(f32[1024,2048]{1,0:T(8,128)S(1)} %fusion.6, bf16[1024,176]{0,1:T(8,128)(2,1)S(1)} %get-tuple-element.17, bf16[1,176,2048]{2,1,0:T(8,128)(2,1)S(1)} %copy-done), kind=kOutput, calls=%fused_computation.9 | convolution fusion | flops 740294656 | bytes 17858560 | tf_op jit(solution)/shard_map/dot_general | solution.py:118
  192.8 0.0 reduce-scatter.5.cloned.1.call-update
  192.8 0.1 reduce_sum.43
  192.9 0.1 dynamic_slice.3
  193.0 85.6 %reduce-scatter.3.cloned.1.call-done = f32[256,1024]{0,1:T(8,128)} async-done(((f32[2048,1024]{0,1:T(8,128)}), f32[256,1024]{0,1:T(8,128)}) %reduce-scatter.3.cloned.1.call-update) | async-done | bytes 1048592 | tf_op jit(solution)/shard_map/reduce_scatter | solution.py:64
  278.6 2.1 multiply_convert_fusion
  280.7 7.4 %all-to-all-start.1 = ((bf16[256,32,32]{0,2,1:T(8,128)(2,1)}), bf16[256,32,32]{0,2,1:T(8,128)(2,1)S(1)}, u32[]{:S(2)}, u32[]{:S(2)}) async-start(bf16[256,32,32]{0,2,1:T(8,128)(2,1)} %bitcast.12), calls=%async_computation.2 | async-start | bytes 1048576 | tf_op jit(solution)/shard_map/all_to_all | solution.py:76
  288.1 0.1 broadcast_in_dim.87
  288.3 0.1 mul.148
  288.4 0.2 mul.149
  288.6 86.1 %reduce-scatter.5.cloned.1.call-done = f32[256,1024]{0,1:T(8,128)} async-done(((f32[2048,1024]{0,1:T(8,128)}), f32[256,1024]{0,1:T(8,128)}) %reduce-scatter.5.cloned.1.call-update) | async-done | bytes 1048592 | tf_op jit(solution)/shard_map/reduce_scatter | solution.py:121
  374.7 0.0 all-to-all-done.1
  374.7 7.4 %all-to-all-start.3 = ((f32[256,32,32]{0,2,1:T(8,128)}), f32[256,32,32]{0,2,1:T(8,128)S(1)}, u32[]{:S(2)}, u32[]{:S(2)}) async-start(f32[256,32,32]{0,2,1:T(8,128)} %bitcast.97), calls=%async_computation.5 | async-start | bytes 2097152 | tf_op jit(solution)/shard_map/all_to_all | solution.py:122
  382.2 4.3 convolution_bitcast_fusion.1
  386.5 4.3 convolution_bitcast_fusion.3
  390.8 4.2 convolution_bitcast_fusion.2
  395.0 1.9 gather_fusion
  397.0 0.1 gather.16
  397.0 0.2 multiply_reduce_fusion
  397.3 0.1 reduce_sum.48
  397.4 28.7 %psum.7 = f32[128,4]{1,0:T(8,128)S(1)} all-reduce(f32[128,4]{1,0:T(8,128)S(1)} %reduce_sum.48), channel_id=1, replica_groups=mesh['dp'=32,'expert'=8] {'expert'}, use_global_device_ids=true, to_apply=%region_11.13 | all-reduce | flops 512 | bytes 4096 | tf_op jit(solution)/shard_map/psum | solution.py:87
  426.1 0.7 copy.24
  426.7 0.0 all-to-all-done.3
  426.7 1.6 gather_fusion.1
  428.3 0.1 gather.18
  428.5 1.4 select_reduce_fusion
  (27 shorter events, 0.2 us)
Async XLA Ops:
  7.2 170.4 %copy-start = (bf16[1,176,2048]{2,1,0:T(8,128)(2,1)S(1)}, bf16[1,176,2048]{2,1,0:T(8,128)(2,1)}, u32[]{:S(2)}) copy-start(bf16[1,176,2048]{2,1,0:T(8,128)(2,1)} %param.16) | copy-start | bytes 2162692
  45.1 6.0 %copy-start.7 = (f32[32,2048]{1,0:T(8,128)S(1)}, f32[32,2048]{1,0:T(8,128)}, u32[]{:S(2)}) copy-start(f32[32,2048]{1,0:T(8,128)} %param.20) | copy-start | bytes 786436
  55.6 7.8 %copy-start.1 = (bf16[128,2048]{1,0:T(8,128)(2,1)S(1)}, bf16[128,2048]{1,0:T(8,128)(2,1)}, u32[]{:S(2)}) copy-start(bf16[128,2048]{1,0:T(8,128)(2,1)} %param.12) | copy-start | bytes 1572868
  55.6 59.2 %all-to-all-start.2 = ((bf16[32,32,2048]{2,1,0:T(8,128)(2,1)}), bf16[32,32,2048]{2,1,0:T(8,128)(2,1)}, u32[]{:S(2)}, u32[]{:S(2)}) async-start(bf16[32,32,2048]{2,1,0:T(8,128)(2,1)} %bitcast.93), calls=%async_computation.3 | async-start | bytes 8388608 | tf_op jit(solution)/shard_map/all_to_all | solution.py:92
  114.9 7.7 %copy-start.5 = (bf16[1,176,2048]{2,1,0:T(8,128)(2,1)S(1)}, bf16[1,176,2048]{2,1,0:T(8,128)(2,1)}, u32[]{:S(2)}) copy-start(bf16[1,176,2048]{2,1,0:T(8,128)(2,1)} %param.17) | copy-start | bytes 2162692
  114.9 58.9 %all-to-all-start = ((bf16[32,32,2048]{2,1,0:T(8,128)(2,1)}), bf16[32,32,2048]{2,1,0:T(8,128)(2,1)}, u32[]{:S(2)}, u32[]{:S(2)}) async-start(bf16[32,32,2048]{2,1,0:T(8,128)(2,1)} %bitcast.92), calls=%async_computation | async-start | bytes 8388608 | tf_op jit(solution)/shard_map/all_to_all | solution.py:43
  122.3 51.5 %copy-start.6 = (bf16[1,176,2048]{2,1,0:T(8,128)(2,1)S(1)}, bf16[1,176,2048]{2,1,0:T(8,128)(2,1)}, u32[]{:S(2)}) copy-start(bf16[1,176,2048]{2,1,0:T(8,128)(2,1)} %param.15) | copy-start | bytes 2162692
  122.3 51.5 %copy-start.9 = (f32[1,176]{1,0:T(1,128)S(1)}, f32[1,176]{1,0:T(1,128)}, u32[]{:S(2)}) copy-start(f32[1,176]{1,0:T(1,128)} %param.18) | copy-start | bytes 2116
  122.3 156.3 %reduce-scatter.3.cloned.1.call-start = ((), (), s32[]{:S(2)}) async-start(), calls=%async_computation.6 | async-start | bytes 9437184 | tf_op jit(solution)/shard_map/reduce_scatter | solution.py:64
  127.1 50.5 %copy-start.10 = (f32[1,176]{1,0:T(1,128)S(1)}, f32[1,176]{1,0:T(1,128)}, u32[]{:S(2)}) copy-start(f32[1,176]{1,0:T(1,128)} %param.19) | copy-start | bytes 2116
  173.8 3.8 copy-start.11
  181.7 0.7 copy-start.2
  181.7 6.6 %copy-start.3 = (bf16[1024,176]{0,1:T(8,128)(2,1)}, bf16[1024,176]{0,1:T(8,128)(2,1)S(1)}, u32[]{:S(2)}) copy-start(bf16[1024,176]{0,1:T(8,128)(2,1)S(1)} %get-tuple-element.17) | copy-start | bytes 1081348
  186.9 187.8 %reduce-scatter.5.cloned.1.call-start = ((), (), s32[]{:S(2)}) async-start(), calls=%async_computation.7 | async-start | bytes 9437184 | tf_op jit(solution)/shard_map/reduce_scatter | solution.py:121
  192.8 95.5 %copy-start.8 = (bf16[128,256]{1,0:T(8,128)(2,1)S(1)}, bf16[128,256]{1,0:T(8,128)(2,1)}, u32[]{:S(2)}) copy-start(bf16[128,256]{1,0:T(8,128)(2,1)} %param.21) | copy-start | bytes 196612
  280.7 94.0 %all-to-all-start.1 = ((bf16[256,32,32]{0,2,1:T(8,128)(2,1)}), bf16[256,32,32]{0,2,1:T(8,128)(2,1)S(1)}, u32[]{:S(2)}, u32[]{:S(2)}) async-start(bf16[256,32,32]{0,2,1:T(8,128)(2,1)} %bitcast.12), calls=%async_computation.2 | async-start | bytes 1048576 | tf_op jit(solution)/shard_map/all_to_all | solution.py:76
  374.7 52.0 %all-to-all-start.3 = ((f32[256,32,32]{0,2,1:T(8,128)}), f32[256,32,32]{0,2,1:T(8,128)S(1)}, u32[]{:S(2)}, u32[]{:S(2)}) async-start(f32[256,32,32]{0,2,1:T(8,128)} %bitcast.97), calls=%async_computation.5 | async-start | bytes 2097152 | tf_op jit(solution)/shard_map/all_to_all | solution.py:122
  386.5 4.3 copy-start.4
Sparse Core Ops, SparseCore 0:
  187.0 91.5 reduce-scatter.2
  281.1 93.5 reduce-scatter.4
where the time goes:
time: 437 us
  waiting for transfers between devices  257 us (59%)
  blocking collectives  58 us (13%)
  matrix products  35.5 us (8%)
  starting transfers between devices  30.3 us (7%)
  local copies, waits for them, and re-layouts  27.5 us (6%)
  between operations  14.4 us (3%)
  other arithmetic  13.6 us (3%)
    reduce_scatter x1, waiting for transfers between devices, local(): lax.psum_scatter(first + second, 'expert', scatter_dimension=0, tiled=True)  86.1 us
    reduce_scatter x1, waiting for transfers between devices, local(): lax.psum_scatter(lax.dot_general(down_local, hidden, (((0,), (1,)), ((),...  85.6 us
    all_to_all x1, waiting for transfers between devices, local(): lax.all_to_all(outgoing.reshape(owners, capacity, width), 'dp', split_axi...  46.7 us
    all_to_all x1, waiting for transfers between devices, local(): lax.all_to_all(weighted.reshape(owners, capacity, width), 'dp', split_axi...  38.9 us
    all_gather x1, blocking collectives, local(): full_cot = lax.all_gather(cotangent, 'expert', axis=1, tiled=True)  29.3 us
    psum x1, blocking collectives, local(): route_grad = lax.psum(route_part, 'expert')  28.7 us
  transfers between devices with their start and end apart: 6, of which 4 were waited for; matrix products, arithmetic and copies ran while one was open for 9% of the time, Pallas kernels for 0%

commit v1 on v0

--- a/solution.py
+++ b/solution.py
@@ -1,7 +1,19 @@
+import functools
 import jax
 import jax.numpy as jnp
 from jax import lax
 from jax.sharding import PartitionSpec as P
+
+
+def attach_loads(message, axis_key):
+    ready = message
+    extent = lax.axis_size(axis_key)
+    for dev_j in [rr for rr in (1, 2, 4, 8, 16) if rr < extent]:
+        ready = ready + lax.ppermute(ready, axis_key, [(k0, k0 ^ dev_j) for k0 in range(extent)])
+    return ready
+
+
+update_the_regions = functools.partial(attach_loads, axis_key="expert")
 
 
 def local(
@@ -84,7 +96,7 @@
     mixed = jnp.sum(picked * route_weight[None, :, :], axis=2).T.astype(jnp.bfloat16)
     cot_cols = cotangent.T.astype(jnp.float32)
     route_part = jnp.sum(picked * cot_cols[:, :, None], axis=0)
-    route_grad = lax.psum(route_part, "expert")
+    route_grad = update_the_regions(route_part)
     slot_scale = jnp.repeat(down_scale, capacity, axis=0)
     full_cot = lax.all_gather(cotangent, "expert", axis=1, tiled=True)
     cot_slots = jnp.take(full_cot, slot_token, axis=0).astype(jnp.float32)

time: 437 us -> 417 us (0.954)
  blocking collectives: 58 us -> 29.3 us
  starting transfers between devices: 30.3 us -> 37.2 us
    psum x1 -> x0, blocking collectives: 28.7 us -> none  [local(): route_grad = lax.psum(route_part, 'expert')]
    ppermute x0 -> x3, starting transfers between devices: none -> 6.84 us  [attach_loads(): lax.ppermute(ready, axis_key, [(k0, k0 ^ dev_j) for k0 in range(extent)])]
  transfers between devices with their start and end apart: 6 -> 9, of which waited for: 4 -> 5; matrix products, arithmetic and copies ran while one was open for 9% -> 10% of each run, Pallas kernels for 0% -> 0%
where the time goes in v1:
time: 417 us; the launch traced here: 416 us
  waiting for transfers between devices  259 us (62%)
  starting transfers between devices  37.2 us (9%)
  matrix products  35.4 us (8%)
  blocking collectives  29.3 us (7%)
  local copies, waits for them, and re-layouts  27.5 us (7%)
  between operations  14.4 us (3%)
  other arithmetic  13.7 us (3%)
    reduce_scatter x1, waiting for transfers between devices, local(): lax.psum_scatter(first + second, 'expert', scatter_dimension=0, tiled=True)  86.1 us
    reduce_scatter x1, waiting for transfers between devices, local(): lax.psum_scatter(lax.dot_general(down_local, hidden, (((0,), (1,)), ((),...  85.6 us
    all_to_all x1, waiting for transfers between devices, local(): lax.all_to_all(outgoing.reshape(owners, capacity, width), 'dp', split_axi...  46.7 us
    all_to_all x1, waiting for transfers between devices, local(): lax.all_to_all(weighted.reshape(owners, capacity, width), 'dp', split_axi...  38.9 us
    all_gather x1, blocking collectives, local(): full_cot = lax.all_gather(cotangent, 'expert', axis=1, tiled=True)  29.3 us
  transfers between devices with their start and end apart: 9, of which 5 were waited for; matrix products, arithmetic and copies ran while one was open for 10% of the time, Pallas kernels for 0%

profile of v1, /device:TPU:2, one launch (start us, length us, event | category | flops | bytes accessed | tf_op | source)
XLA Modules:
  0.0 416.1 jit_solution(18142154918511861397)
XLA Ops:
  7.2 0.0 copy-start
  7.2 0.9 copy.18
  8.0 0.1 eq.26
  8.2 0.1 reshape.136
  8.3 1.2 reduce-window.6
  9.5 0.2 slice_reduce_fusion
  9.7 0.1 mul.123
  9.8 0.1 fusion.11
  10.0 2.4 scatter_custom_fusion.1
  12.4 0.8 copy.22
  13.2 0.1 reshape.200
  13.3 29.3 %all_gather.3 = bf16[128,2048]{1,0:T(8,128)(2,1)S(1)} all-gather(bf16[128,256]{1,0:T(8,128)(2,1)} %param.21), channel_id=1, replica_groups=mesh['dp'=32,'expert'=8] {'expert'}, dimensions={1}, use_global_device_ids=true | all-gather | bytes 589824 | tf_op jit(solution)/shard_map/all_gather | solution.py:101
  42.7 2.4 scatter_custom_fusion.2
  45.1 0.0 copy-start.7
  45.1 6.0 %gather_fusion.3 = bf16[1024,2048]{1,0:T(8,128)(2,1)} fusion(bf16[128,2048]{1,0:T(8,128)(2,1)S(1)} %all_gather.3, s32[1024]{0:T(1024)S(1)} %fusion.13), kind=kCustom, calls=%fused_computation.1.clone | custom fusion | bytes 8392704 | tf_op jit(solution)/shard_map/jit(_take)/gather | solution.py:102
  51.2 4.5 %fusion = bf16[1024,2048]{1,0:T(8,128)(2,1)} fusion(bf16[1024,2048]{1,0:T(8,128)(2,1)} %gather_fusion.3, f32[32,2048]{1,0:T(8,128)S(1)} %copy-done.7, f32[1024]{0:T(1024)S(1)} %scatter_custom_fusion.2, pred[1024]{0:T(1024)(128)(4,1)S(1)} %compare_and_fusion.1), kind=kLoop, calls=%fused_computation.8 | loop fusion | flops 10485760 | bytes 8655872 | tf_op jit(solution)/shard_map/convert_element_type | solution.py:103
  55.6 7.8 %all-to-all-start.2 = ((bf16[32,32,2048]{2,1,0:T(8,128)(2,1)}), bf16[32,32,2048]{2,1,0:T(8,128)(2,1)}, u32[]{:S(2)}, u32[]{:S(2)}) async-start(bf16[32,32,2048]{2,1,0:T(8,128)(2,1)} %bitcast.93), calls=%async_computation.3 | async-start | bytes 8388608 | tf_op jit(solution)/shard_map/all_to_all | solution.py:104
  63.4 6.0 %gather_fusion.2 = bf16[1024,2048]{1,0:T(8,128)(2,1)} fusion(bf16[128,2048]{1,0:T(8,128)(2,1)S(1)} %copy-done.1, s32[1024]{0:T(1024)S(1)} %fusion.13), kind=kCustom, calls=%fused_computation.clone | custom fusion | bytes 8392704 | tf_op jit(solution)/shard_map/jit(_take)/gather | solution.py:53
  69.5 2.4 scatter_custom_fusion
  71.9 4.0 select_select_fusion
  75.9 38.9 %all-to-all-done.2 = bf16[32,32,2048]{2,1,0:T(8,128)(2,1)} async-done(((bf16[32,32,2048]{2,1,0:T(8,128)(2,1)}), bf16[32,32,2048]{2,1,0:T(8,128)(2,1)}, u32[]{:S(2)}, u32[]{:S(2)}) %all-to-all-start.2) | async-done | bytes 4194336 | tf_op jit(solution)/shard_map/all_to_all | solution.py:104
  114.9 7.4 %all-to-all-start = ((bf16[32,32,2048]{2,1,0:T(8,128)(2,1)}), bf16[32,32,2048]{2,1,0:T(8,128)(2,1)}, u32[]{:S(2)}, u32[]{:S(2)}) async-start(bf16[32,32,2048]{2,1,0:T(8,128)(2,1)} %bitcast.92), calls=%async_computation | async-start | bytes 8388608 | tf_op jit(solution)/shard_map/all_to_all | solution.py:55
  122.3 0.0 copy-start.6
  122.3 0.0 copy-start.9
  122.3 0.2 reduce-scatter.3.cloned.1.call-start
  122.5 4.6 %fusion.1 = f32[1024,176]{0,1:T(8,128)} fusion(bf16[1024,2048]{1,0:T(8,128)(2,1)} %bitcast.18, bf16[1,176,2048]{2,1,0:T(8,128)(2,1)S(1)} %copy-done.5), kind=kOutput, calls=%fused_computation.18 | convolution fusion | flops 738197504 | bytes 5636096 | tf_op jit(solution)/shard_map/dot_general | solution.py:107
  127.1 46.7 %all-to-all-done = bf16[32,32,2048]{2,1,0:T(8,128)(2,1)} async-done(((bf16[32,32,2048]{2,1,0:T(8,128)(2,1)}), bf16[32,32,2048]{2,1,0:T(8,128)(2,1)}, u32[]{:S(2)}, u32[]{:S(2)}) %all-to-all-start) | async-done | bytes 4194336 | tf_op jit(solution)/shard_map/all_to_all | solution.py:55
  173.8 3.8 convolution_multiply_fusion.1
  177.6 4.0 multiply_convert_fusion.3
  181.7 0.0 copy-start.2
  181.7 0.0 copy-start.3
  181.7 0.7 copy-done.2
  182.4 4.5 %convolution_bitcast_fusion = f32[2048,1024]{0,1:T(8,128)} fusion(bf16[1024,176]{0,1:T(8,128)(2,1)S(1)} %get-tuple-element.15, bf16[1,176,2048]{2,1,0:T(8,128)(2,1)S(1)} %copy-done.5), kind=kOutput, calls=%fused_computation.10 | convolution fusion | flops 738197504 | bytes 9469952 | tf_op jit(solution)/shard_map/dot_general | solution.py:77
  186.9 0.0 reduce-scatter.3.cloned.1.call-update
  186.9 0.0 reduce-scatter.5.cloned.1.call-start
  187.0 1.3 fusion.6
  188.3 4.5 %add_bitcast_fusion = f32[2048,1024]{0,1:T(8,128)} fusion(f32[1024,2048]{1,0:T(8,128)S(1)} %fusion.6, bf16[1024,176]{0,1:T(8,128)(2,1)S(1)} %get-tuple-element.17, bf16[1,176,2048]{2,1,0:T(8,128)(2,1)S(1)} %copy-done), kind=kOutput, calls=%fused_computation.9 | convolution fusion | flops 740294656 | bytes 17858560 | tf_op jit(solution)/shard_map/dot_general | solution.py:130
  192.8 0.0 reduce-scatter.5.cloned.1.call-update
  192.8 0.1 reduce_sum.43
  192.9 0.1 dynamic_slice.3
  193.0 85.6 %reduce-scatter.3.cloned.1.call-done = f32[256,1024]{0,1:T(8,128)} async-done(((f32[2048,1024]{0,1:T(8,128)}), f32[256,1024]{0,1:T(8,128)}) %reduce-scatter.3.cloned.1.call-update) | async-done | bytes 1048592 | tf_op jit(solution)/shard_map/reduce_scatter | solution.py:76
  278.6 2.1 multiply_convert_fusion
  280.7 7.4 %all-to-all-start.1 = ((bf16[256,32,32]{0,2,1:T(8,128)(2,1)}), bf16[256,32,32]{0,2,1:T(8,128)(2,1)S(1)}, u32[]{:S(2)}, u32[]{:S(2)}) async-start(bf16[256,32,32]{0,2,1:T(8,128)(2,1)} %bitcast.12), calls=%async_computation.2 | async-start | bytes 1048576 | tf_op jit(solution)/shard_map/all_to_all | solution.py:88
  288.1 0.1 broadcast_in_dim.87
  288.3 0.1 mul.148
  288.4 0.2 mul.149
  288.6 86.1 %reduce-scatter.5.cloned.1.call-done = f32[256,1024]{0,1:T(8,128)} async-done(((f32[2048,1024]{0,1:T(8,128)}), f32[256,1024]{0,1:T(8,128)}) %reduce-scatter.5.cloned.1.call-update) | async-done | bytes 1048592 | tf_op jit(solution)/shard_map/reduce_scatter | solution.py:133
  374.7 7.4 %all-to-all-start.3 = ((f32[256,32,32]{0,2,1:T(8,128)}), f32[256,32,32]{0,2,1:T(8,128)S(1)}, u32[]{:S(2)}, u32[]{:S(2)}) async-start(f32[256,32,32]{0,2,1:T(8,128)} %bitcast.97), calls=%async_computation.5 | async-start | bytes 2097152 | tf_op jit(solution)/shard_map/all_to_all | solution.py:134
  382.2 2.0 gather_fusion
  384.1 0.2 multiply_reduce_fusion
  384.4 0.1 reduce_sum.48
  384.5 0.1 collective-permute-start
  384.6 4.3 %convolution_bitcast_fusion.1 = f32[1,176,2048]{2,1,0:T(8,128)} fusion(bf16[1024,176]{0,1:T(8,128)(2,1)} %copy-done.2, bf16[1024,2048]{1,0:T(8,128)(2,1)} %bitcast.18), kind=kOutput, calls=%fused_computation.12 | convolution fusion | flops 738197504 | bytes 5996544 | tf_op jit(solution)/shard_map/dot_general | solution.py:118
  388.9 3.8 collective-permute-start.1
  392.8 4.2 %convolution_bitcast_fusion.3 = f32[1,176,2048]{2,1,0:T(8,128)} fusion(bf16[1024,176]{0,1:T(8,128)(2,1)S(1)} %get-tuple-element.16, bf16[1024,2048]{1,0:T(8,128)(2,1)} %bitcast.4), kind=kOutput, calls=%fused_computation.14 | convolution fusion | flops 738197504 | bytes 5996544 | tf_op jit(solution)/shard_map/dot_general | solution.py:121
  397.0 0.0 collective-permute-done.1
  397.0 2.9 collective-permute-start.2
  399.9 4.2 %convolution_bitcast_fusion.2 = f32[1,176,2048]{2,1,0:T(8,128)} fusion(bf16[1024,176]{0,1:T(8,128)(2,1)S(1)} %copy-done.4, bf16[1024,2048]{1,0:T(8,128)(2,1)} %bitcast.4), kind=kOutput, calls=%fused_computation.13 | convolution fusion | flops 738197504 | bytes 5996544 | tf_op jit(solution)/shard_map/dot_general | solution.py:124
  404.1 0.1 gather.16
  404.2 1.3 collective-permute-done.2
  405.5 0.7 copy.24
  406.1 1.6 gather_fusion.1
  407.7 0.1 gather.18
  407.8 1.4 select_reduce_fusion
  (35 shorter events, 0.2 us)
Async XLA Ops:
  7.2 170.4 %copy-start = (bf16[1,176,2048]{2,1,0:T(8,128)(2,1)S(1)}, bf16[1,176,2048]{2,1,0:T(8,128)(2,1)}, u32[]{:S(2)}) copy-start(bf16[1,176,2048]{2,1,0:T(8,128)(2,1)} %param.16) | copy-start | bytes 2162692
  45.1 6.0 %copy-start.7 = (f32[32,2048]{1,0:T(8,128)S(1)}, f32[32,2048]{1,0:T(8,128)}, u32[]{:S(2)}) copy-start(f32[32,2048]{1,0:T(8,128)} %param.20) | copy-start | bytes 786436
  55.6 7.8 %copy-start.1 = (bf16[128,2048]{1,0:T(8,128)(2,1)S(1)}, bf16[128,2048]{1,0:T(8,128)(2,1)}, u32[]{:S(2)}) copy-start(bf16[128,2048]{1,0:T(8,128)(2,1)} %param.12) | copy-start | bytes 1572868
  55.6 59.2 %all-to-all-start.2 = ((bf16[32,32,2048]{2,1,0:T(8,128)(2,1)}), bf16[32,32,2048]{2,1,0:T(8,128)(2,1)}, u32[]{:S(2)}, u32[]{:S(2)}) async-start(bf16[32,32,2048]{2,1,0:T(8,128)(2,1)} %bitcast.93), calls=%async_computation.3 | async-start | bytes 8388608 | tf_op jit(solution)/shard_map/all_to_all | solution.py:104
  114.9 7.7 %copy-start.5 = (bf16[1,176,2048]{2,1,0:T(8,128)(2,1)S(1)}, bf16[1,176,2048]{2,1,0:T(8,128)(2,1)}, u32[]{:S(2)}) copy-start(bf16[1,176,2048]{2,1,0:T(8,128)(2,1)} %param.17) | copy-start | bytes 2162692
  114.9 58.9 %all-to-all-start = ((bf16[32,32,2048]{2,1,0:T(8,128)(2,1)}), bf16[32,32,2048]{2,1,0:T(8,128)(2,1)}, u32[]{:S(2)}, u32[]{:S(2)}) async-start(bf16[32,32,2048]{2,1,0:T(8,128)(2,1)} %bitcast.92), calls=%async_computation | async-start | bytes 8388608 | tf_op jit(solution)/shard_map/all_to_all | solution.py:55
  122.3 51.5 %copy-start.6 = (bf16[1,176,2048]{2,1,0:T(8,128)(2,1)S(1)}, bf16[1,176,2048]{2,1,0:T(8,128)(2,1)}, u32[]{:S(2)}) copy-start(bf16[1,176,2048]{2,1,0:T(8,128)(2,1)} %param.15) | copy-start | bytes 2162692
  122.3 51.5 %copy-start.9 = (f32[1,176]{1,0:T(1,128)S(1)}, f32[1,176]{1,0:T(1,128)}, u32[]{:S(2)}) copy-start(f32[1,176]{1,0:T(1,128)} %param.18) | copy-start | bytes 2116
  122.3 156.3 %reduce-scatter.3.cloned.1.call-start = ((), (), s32[]{:S(2)}) async-start(), calls=%async_computation.6 | async-start | bytes 9437184 | tf_op jit(solution)/shard_map/reduce_scatter | solution.py:76
  127.1 50.5 %copy-start.10 = (f32[1,176]{1,0:T(1,128)S(1)}, f32[1,176]{1,0:T(1,128)}, u32[]{:S(2)}) copy-start(f32[1,176]{1,0:T(1,128)} %param.19) | copy-start | bytes 2116
  173.8 3.8 copy-start.11
  181.7 0.7 copy-start.2
  181.7 6.6 %copy-start.3 = (bf16[1024,176]{0,1:T(8,128)(2,1)}, bf16[1024,176]{0,1:T(8,128)(2,1)S(1)}, u32[]{:S(2)}) copy-start(bf16[1024,176]{0,1:T(8,128)(2,1)S(1)} %get-tuple-element.17) | copy-start | bytes 1081348
  186.9 187.8 %reduce-scatter.5.cloned.1.call-start = ((), (), s32[]{:S(2)}) async-start(), calls=%async_computation.7 | async-start | bytes 9437184 | tf_op jit(solution)/shard_map/reduce_scatter | solution.py:133
  192.8 95.5 %copy-start.8 = (bf16[128,256]{1,0:T(8,128)(2,1)S(1)}, bf16[128,256]{1,0:T(8,128)(2,1)}, u32[]{:S(2)}) copy-start(bf16[128,256]{1,0:T(8,128)(2,1)} %param.21) | copy-start | bytes 196612
  280.7 94.0 %all-to-all-start.1 = ((bf16[256,32,32]{0,2,1:T(8,128)(2,1)}), bf16[256,32,32]{0,2,1:T(8,128)(2,1)S(1)}, u32[]{:S(2)}, u32[]{:S(2)}) async-start(bf16[256,32,32]{0,2,1:T(8,128)(2,1)} %bitcast.12), calls=%async_computation.2 | async-start | bytes 1048576 | tf_op jit(solution)/shard_map/all_to_all | solution.py:88
  374.7 31.4 %all-to-all-start.3 = ((f32[256,32,32]{0,2,1:T(8,128)}), f32[256,32,32]{0,2,1:T(8,128)S(1)}, u32[]{:S(2)}, u32[]{:S(2)}) async-start(f32[256,32,32]{0,2,1:T(8,128)} %bitcast.97), calls=%async_computation.5 | async-start | bytes 2097152 | tf_op jit(solution)/shard_map/all_to_all | solution.py:134
  384.5 4.4 %collective-permute-start = (f32[128,4]{1,0:T(8,128)S(1)}, f32[128,4]{1,0:T(8,128)S(1)}, u32[]{:S(2)}, u32[]{:S(2)}) collective-permute-start(f32[128,4]{1,0:T(8,128)S(1)} %reduce_sum.48), channel_id=1, source_target_pairs={{0,1},{1,0},{2,3},{3,2},{4,5},{5,4},{6,7},{7,6},{8,9},{9,8},{10,11... | collective-permute-start | bytes 6152 | tf_op jit(solution)/shard_map/ppermute | solution.py:12
  388.9 11.0 %copy-start.4 = (bf16[1024,176]{0,1:T(8,128)(2,1)S(1)}, bf16[1024,176]{0,1:T(8,128)(2,1)}, u32[]{:S(2)}) copy-start(bf16[1024,176]{0,1:T(8,128)(2,1)} %copy-done.3) | copy-start | bytes 1081348
  388.9 8.0 %collective-permute-start.1 = (f32[128,4]{1,0:T(8,128)S(1)}, f32[128,4]{1,0:T(8,128)S(1)}, u32[]{:S(2)}, u32[]{:S(2)}) collective-permute-start(f32[128,4]{1,0:T(8,128)S(1)} %add.97), channel_id=1, source_target_pairs={{0,2},{1,3},{2,0},{3,1},{4,6},{5,7},{6,4},{7,5},{8,10},{9,11},{10,... | collective-permute-start | bytes 6152 | tf_op jit(solution)/shard_map/ppermute | solution.py:12
  397.0 8.4 %collective-permute-start.2 = (f32[128,4]{1,0:T(8,128)S(1)}, f32[128,4]{1,0:T(8,128)S(1)}, u32[]{:S(2)}, u32[]{:S(2)}) collective-permute-start(f32[128,4]{1,0:T(8,128)S(1)} %add.98), channel_id=1, source_target_pairs={{0,4},{1,5},{2,6},{3,7},{4,0},{5,1},{6,2},{7,3},{8,12},{9,13},{10,... | collective-permute-start | bytes 6152 | tf_op jit(solution)/shard_map/ppermute | solution.py:12
Sparse Core Ops, SparseCore 0:
  187.0 91.5 reduce-scatter.2
  281.1 93.5 reduce-scatter.4
